TPU v7x, 512 devices: a whole 4x4x16 slice. The times are simulated.
512 devices in a mesh: dp: 32 (over z, y_hi), seq: 16 (over y_lo, x, core).
Axes of the slice: x: 4, y: 4 (y_hi: 2, y_lo: 2; y = y_hi * 2 + y_lo), z: 16, core: 2. Of those that a mesh axis runs over, the one named last changes fastest.
Arguments:
- sequence_in: bfloat16 [32, 8192, 768], P('dp', 'seq'), may hold values from -6 to 6
- output_grad: bfloat16 [32, 8192, 768], P('dp', 'seq'), may hold values from -6 to 6
- skip_mask: int32 [32, 2], P('dp'), may hold values 0 or 1
- in_gain: float32 [2, 768], replicated, may hold values from 0.25 to 1.75
- input_shift_vec: float32 [2, 768], replicated, may hold values from -3 to 3
- mid_gain: float32 [2, 384], replicated, may hold values from 0.25 to 1.75
- mid_offset: float32 [2, 384], replicated, may hold values from -3 to 3
- conv_weight: bfloat16 [2, 3, 768, 384], P(None, None, 'seq'), may hold values from -0.21875 to 0.21875
- point_weight: bfloat16 [384, 2, 768], P('seq'), may hold values from -0.3125 to 0.3125
Outputs:
- point_grad: float32 [384, 2, 768], P('seq')
- input_grad: bfloat16 [32, 8192, 768], P('dp', 'seq')
Inputs may be any that keep to these rules, and one draw needn't show every extreme that they name: skip_mask[s, b] = 1 means that sample s passes block b unchanged in this step.
All inputs are finite; a program needn't handle non-finite values.
Results may differ from a plain program's by a relative error of at most 0.009.
Values may be sent and summed in bfloat16 or wider, within the bound.
No kernel may reach another device: no remote copies, remote signals or barrier semaphores. Data moves between devices by JAX's collectives and lax.ppermute only.
A program may use at most 64 MiB of HBM per device.

v0:
```python
import math
import jax
import jax.numpy as jnp
from jax import lax
from jax.sharding import PartitionSpec as P

FIRST_DILATION = 1024
SECOND_DILATION = 2048


def passed_along(value, axis, by):
    peers = lax.axis_size(axis)
    pairs = [(i, i + by) for i in range(peers) if 0 <= i + by < peers]
    return lax.ppermute(value, axis, pairs)


def gelu_tanh(values):
    return jax.nn.gelu(values, approximate=True)


def contract_last(left, right):
    return lax.dot_general(
        left, right, (((1,), (1,)), ((), ())), preferred_element_type=jnp.float32
    )


def neighbours(source, shards_away):
    earlier = passed_along(source, "seq", shards_away)
    later = passed_along(source, "seq", -shards_away)
    return (earlier, later)


def forward_local(
    state, earlier, activated, later, weight, gain_vec, offset_vec, projection, kept_flag
):
    conv_out = jnp.dot(earlier, weight[0], preferred_element_type=jnp.float32)
    conv_out = conv_out + jnp.dot(activated, weight[1], preferred_element_type=jnp.float32)
    conv_out = conv_out + jnp.dot(later, weight[2], preferred_element_type=jnp.float32)
    middle = conv_out * gain_vec + offset_vec
    hidden_act = gelu_tanh(middle).astype(jnp.bfloat16)
    branch = jnp.dot(hidden_act, projection, preferred_element_type=jnp.float32)
    result = (state.astype(jnp.float32) + kept_flag * branch).astype(jnp.bfloat16)
    return (middle, hidden_act, result)


def backward_first(gradient, middle, projection, gain_vec, kept_flag):
    branch_grad = (kept_flag * gradient.astype(jnp.float32)).astype(jnp.bfloat16)
    hidden_grad = contract_last(branch_grad, projection)
    middle_grad = jax.vjp(gelu_tanh, middle)[1](hidden_grad)[0]
    conv_grad = (middle_grad * gain_vec).astype(jnp.bfloat16)
    return (conv_grad, branch_grad)


def backward_second(gradient, earlier, conv_grad, later, weight, normed, gain_vec):
    act_grad = (
        contract_last(later, weight[0])
        + contract_last(conv_grad, weight[1])
        + contract_last(earlier, weight[2])
    )
    normed_grad = jax.vjp(gelu_tanh, normed)[1](act_grad)[0] * gain_vec
    return (gradient.astype(jnp.float32) + normed_grad).astype(jnp.bfloat16)


def grad_rows(hidden_act, branch_grad):
    return lax.dot_general(
        hidden_act, branch_grad, (((0,), (0,)), ((), ())), preferred_element_type=jnp.float32
    )


def shards(
    sequence_in,
    output_grad,
    skip_mask,
    in_gain,
    input_shift_vec,
    mid_gain,
    mid_offset,
    conv_weight,
    point_weight,
):
    position_list = sequence_in.shape[1]
    channels = sequence_in.shape[2]
    point_full = lax.all_gather(point_weight, "seq", axis=0, tiled=True)
    neighbour_reach = (FIRST_DILATION // position_list, SECOND_DILATION // position_list)
    state = sequence_in.reshape(-1, channels)
    total_rows = state.shape[0]
    saved = []
    kept_weights = []
    for block_index in range(2):
        kept_flag = (1 - skip_mask[0, block_index]).astype(jnp.float32)
        normed = state.astype(jnp.float32) * in_gain[block_index] + input_shift_vec[block_index]
        activated = gelu_tanh(normed).astype(jnp.bfloat16)
        earlier, later = neighbours(
            activated.reshape(sequence_in.shape), neighbour_reach[block_index]
        )
        earlier = earlier.reshape(total_rows, channels)
        later = later.reshape(total_rows, channels)
        weight = lax.all_gather(conv_weight[block_index], "seq", axis=1, tiled=True)
        kept_weights.append(weight)
        operands = (
            state,
            earlier,
            activated,
            later,
            weight,
            mid_gain[block_index],
            mid_offset[block_index],
            point_full[:, block_index, :],
            kept_flag,
        )
        middle, hidden_act, state = forward_local(*operands)
        saved.append((normed, middle, hidden_act, kept_flag))
    gradient = output_grad.reshape(-1, channels)
    hidden_saved = [None, None]
    branch_saved = [None, None]
    for block_index in (1, 0):
        normed, middle, hidden_act, kept_flag = saved[block_index]
        projection = point_full[:, block_index, :]
        first_operands = (gradient, middle, projection, mid_gain[block_index], kept_flag)
        conv_grad, branch_grad = backward_first(*first_operands)
        hidden_saved[block_index] = hidden_act
        branch_saved[block_index] = branch_grad
        earlier, later = neighbours(
            conv_grad.reshape(sequence_in.shape[0], position_list, -1), neighbour_reach[block_index]
        )
        earlier = earlier.reshape(total_rows, -1)
        later = later.reshape(total_rows, -1)
        weight = lax.all_gather(conv_weight[block_index], "seq", axis=1, tiled=True)
        second_operands = (
            gradient,
            earlier,
            conv_grad,
            later,
            weight,
            normed,
            in_gain[block_index],
        )
        gradient = backward_second(*second_operands)
    first_term = grad_rows(hidden_saved[0], branch_saved[0])
    second_term = grad_rows(hidden_saved[1], branch_saved[1])
    shared_part = lax.psum_scatter(
        jnp.stack([first_term, second_term], axis=1), "seq", scatter_dimension=0, tiled=True
    )
    summed = lax.psum(shared_part, "dp")
    sample_count = sequence_in.shape[0] * lax.axis_size("dp")
    full_length = position_list * lax.axis_size("seq")
    point_grad = summed * (1.0 / math.sqrt(sample_count * full_length))
    return (point_grad, gradient.reshape(sequence_in.shape))


def solution(mesh):
    return jax.shard_map(
        shards,
        mesh=mesh,
        in_specs=(
            P("dp", "seq", None),
            P("dp", "seq", None),
            P("dp", None),
            P(),
            P(),
            P(),
            P(),
            P(None, None, "seq", None),
            P("seq", None, None),
        ),
        out_specs=(P("seq", None, None), P("dp", "seq", None)),
        check_vma=False,
    )
```

profile of v0, /device:TPU:2, one launch (start us, length us, event | category | flops | bytes accessed | tf_op | source)
XLA Modules:
  0.0 578.6 jit_solution(11100754376341167043)
XLA Ops:
  7.2 1.7 fusion.103
  12.1 1.8 fusion.15
  13.9 7.8 %collective-permute-start.1 = (bf16[1,512,768]{2,1,0:T(8,128)(2,1)S(1)}, bf16[1,512,768]{2,1,0:T(8,128)(2,1)S(1)}, u32[]{:S(2)}, u32[]{:S(2)}) collective-permute-start(bf16[1,512,768]{2,1,0:T(8,128)(2,1)S(1)} %fusion.15), channel_id=1, source_target_pairs={{2,0},{3,1},{4,2},{5,3},{6,4},{7,5},{8,6},{9,7},{10,8},{11,9},{12,... | collective-permute-start | bytes 2359304 | tf_op jit(solution)/shard_map/ppermute | solution.py:14
  21.7 1.9 collective-permute-start
  25.0 37.8 %all-gather.8.cloned.1.call-done = bf16[1,3,768,384]{3,2,1,0:T(8,128)(2,1)} async-done(((bf16[1,3,48,384]{3,2,1,0:T(8,128)(2,1)}), bf16[1,3,768,384]{3,2,1,0:T(8,128)(2,1)}) %all-gather.8.cloned.1.call-update) | async-done | bytes 1769488 | tf_op jit(solution)/shard_map/all_gather | solution.py:98
  62.7 1.8 fusion.70
  65.1 2.7 fusion.44
  67.8 40.6 %all-gather.6.cloned.1.call-done = bf16[384,2,768]{2,0,1:T(8,128)(2,1)} async-done(((bf16[24,2,768]{2,0,1:T(8,128)(2,1)}), bf16[384,2,768]{2,0,1:T(8,128)(2,1)}) %all-gather.6.cloned.1.call-update) | async-done | bytes 1179664 | tf_op jit(solution)/shard_map/all_gather | solution.py:83
  108.3 2.0 fusion.4
  112.3 7.0 %collective-permute-start.2 = (bf16[1,512,768]{2,1,0:T(8,128)(2,1)S(1)}, bf16[1,512,768]{2,1,0:T(8,128)(2,1)}, u32[]{:S(2)}, u32[]{:S(2)}) collective-permute-start(bf16[1,512,768]{2,1,0:T(8,128)(2,1)S(1)} %fusion.102), channel_id=1, source_target_pairs={{0,4},{1,5},{2,6},{3,7},{4,8},{5,9},{6,10},{7,11},{8,12},{9,13},{1... | collective-permute-start | bytes 2359304 | tf_op jit(solution)/shard_map/ppermute | solution.py:14
  119.8 41.1 %all-gather.10.cloned.1.call-done = bf16[1,3,768,384]{3,2,1,0:T(8,128)(2,1)} async-done(((bf16[1,3,48,384]{3,2,1,0:T(8,128)(2,1)}), bf16[1,3,768,384]{3,2,1,0:T(8,128)(2,1)}) %all-gather.10.cloned.1.call-update) | async-done | bytes 1769488 | tf_op jit(solution)/shard_map/all_gather | solution.py:98
  160.9 2.0 fusion.88
  162.9 1.7 fusion.65
  164.7 1.9 fusion.41
  168.8 6.1 %collective-permute-start.5 = (bf16[1,512,384]{2,1,0:T(8,128)(2,1)S(1)}, bf16[1,512,384]{2,1,0:T(8,128)(2,1)S(1)}, u32[]{:S(2)}, u32[]{:S(2)}) collective-permute-start(bf16[1,512,384]{2,1,0:T(8,128)(2,1)S(1)} %bitcast.137), channel_id=1, source_target_pairs={{0,4},{1,5},{2,6},{3,7},{4,8},{5,9},{6,10},{7,11},{8,12},{9,13},{1... | collective-permute-start | bytes 1179656 | tf_op jit(solution)/shard_map/ppermute | solution.py:14
  176.2 6.6 %collective-permute-done.4 = bf16[1,512,384]{2,1,0:T(8,128)(2,1)S(1)} collective-permute-done((bf16[1,512,384]{2,1,0:T(8,128)(2,1)S(1)}, bf16[1,512,384]{2,1,0:T(8,128)(2,1)S(1)}, u32[]{:S(2)}, u32[]{:S(2)}) %collective-permute-start.4) | collective-permute-done | bytes 393248 | tf_op jit(solution)/shard_map/ppermute | solution.py:14
  188.7 2.8 fusion.52
  191.5 1.9 collective-permute-start.6
  193.4 4.6 collective-permute-start.7
  199.6 5.2 collective-permute-done.6
  204.8 1.7 fusion.83
  206.5 55.3 %reduce-scatter.2.cloned.1.call-done = f32[24,2,768]{2,0,1:T(8,128)} async-done(((f32[384,2,768]{2,0,1:T(8,128)}), f32[24,2,768]{2,0,1:T(8,128)}) %reduce-scatter.2.cloned.1.call-update) | async-done | bytes 147472 | tf_op jit(solution)/shard_map/reduce_scatter | solution.py:141
  261.9 4.5 fusion.77
  266.4 304.0 %all-reduce.2.cloned.1.call-done = f32[24,2,768]{2,0,1:T(8,128)} async-done(((f32[24,2,768]{2,0,1:T(8,128)}), f32[24,2,768]{2,0,1:T(8,128)}) %all-reduce.2.cloned.1.call-update) | async-done | bytes 147472 | tf_op jit(solution)/shard_map/psum | solution.py:144
  (56 shorter events, 19.0 us)
Async XLA Ops:
  7.2 16.5 %copy-start.6 = (s32[1,2]{1,0:T(1,128)S(1)}, s32[1,2]{1,0:T(1,128)}, u32[]{:S(2)}) copy-start(s32[1,2]{1,0:T(1,128)} %param.11) | copy-start | bytes 28
  7.2 17.7 %copy-start.5 = (f32[2,384]{1,0:T(2,128)S(1)}, f32[2,384]{1,0:T(2,128)}, u32[]{:S(2)}) copy-start(f32[2,384]{1,0:T(2,128)} %param.14) | copy-start | bytes 9220
  7.2 17.7 %copy-start.4 = (f32[2,384]{1,0:T(2,128)S(1)}, f32[2,384]{1,0:T(2,128)}, u32[]{:S(2)}) copy-start(f32[2,384]{1,0:T(2,128)} %param.15) | copy-start | bytes 9220
  7.2 55.5 %all-gather.8.cloned.1.call-start = ((), (), s32[]{:S(2)}) async-start(), calls=%async_computation.4 | async-start | bytes 1880064 | tf_op jit(solution)/shard_map/all_gather | solution.py:98
  8.9 99.4 %all-gather.6.cloned.1.call-start = ((), (), s32[]{:S(2)}) async-start(), calls=%async_computation.1 | async-start | bytes 1253376 | tf_op jit(solution)/shard_map/all_gather | solution.py:83
  10.5 150.4 %all-gather.10.cloned.1.call-start = ((), (), s32[]{:S(2)}) async-start(), calls=%async_computation.5 | async-start | bytes 1880064 | tf_op jit(solution)/shard_map/all_gather | solution.py:98
  11.3 250.6 %reduce-scatter.2.cloned.1.call-start = ((), (), s32[]{:S(2)}) async-start(), calls=%async_computation.2 | async-start | bytes 2506752 | tf_op jit(solution)/shard_map/reduce_scatter | solution.py:141
  13.9 50.6 %collective-permute-start.1 = (bf16[1,512,768]{2,1,0:T(8,128)(2,1)S(1)}, bf16[1,512,768]{2,1,0:T(8,128)(2,1)S(1)}, u32[]{:S(2)}, u32[]{:S(2)}) collective-permute-start(bf16[1,512,768]{2,1,0:T(8,128)(2,1)S(1)} %fusion.15), channel_id=1, source_target_pairs={{2,0},{3,1},{4,2},{5,3},{6,4},{7,5},{8,6},{9,7},{10,8},{11,9},{12,... | collective-permute-start | bytes 2359304 | tf_op jit(solution)/shard_map/ppermute | solution.py:14
  21.7 43.3 %collective-permute-start = (bf16[1,512,768]{2,1,0:T(8,128)(2,1)S(1)}, bf16[1,512,768]{2,1,0:T(8,128)(2,1)}, u32[]{:S(2)}, u32[]{:S(2)}) collective-permute-start(bf16[1,512,768]{2,1,0:T(8,128)(2,1)S(1)} %fusion.15), channel_id=1, source_target_pairs={{0,2},{1,3},{2,4},{3,5},{4,6},{5,7},{6,8},{7,9},{8,10},{9,11},{10,... | collective-permute-start | bytes 2359304 | tf_op jit(solution)/shard_map/ppermute | solution.py:14
  62.7 1.8 copy-start
  65.1 43.3 %copy-start.2 = (bf16[1,512,768]{2,1,0:T(8,128)(2,1)S(1)}, bf16[1,512,768]{2,1,0:T(8,128)(2,1)}, u32[]{:S(2)}) copy-start(bf16[1,512,768]{2,1,0:T(8,128)(2,1)} %param.9) | copy-start | bytes 2359300
  111.0 51.9 %collective-permute-start.3 = (bf16[1,512,768]{2,1,0:T(8,128)(2,1)S(1)}, bf16[1,512,768]{2,1,0:T(8,128)(2,1)}, u32[]{:S(2)}, u32[]{:S(2)}) collective-permute-start(bf16[1,512,768]{2,1,0:T(8,128)(2,1)S(1)} %fusion.102), channel_id=1, source_target_pairs={{4,0},{5,1},{6,2},{7,3},{8,4},{9,5},{10,6},{11,7},{12,8},{13,9},{1... | collective-permute-start | bytes 2359304 | tf_op jit(solution)/shard_map/ppermute | solution.py:14
  112.3 52.4 %collective-permute-start.2 = (bf16[1,512,768]{2,1,0:T(8,128)(2,1)S(1)}, bf16[1,512,768]{2,1,0:T(8,128)(2,1)}, u32[]{:S(2)}, u32[]{:S(2)}) collective-permute-start(bf16[1,512,768]{2,1,0:T(8,128)(2,1)S(1)} %fusion.102), channel_id=1, source_target_pairs={{0,4},{1,5},{2,6},{3,7},{4,8},{5,9},{6,10},{7,11},{8,12},{9,13},{1... | collective-permute-start | bytes 2359304 | tf_op jit(solution)/shard_map/ppermute | solution.py:14
  160.9 2.0 copy-start.1
  164.7 1.9 copy-start.7
  164.7 1.9 copy-start.8
  167.5 15.3 %collective-permute-start.4 = (bf16[1,512,384]{2,1,0:T(8,128)(2,1)S(1)}, bf16[1,512,384]{2,1,0:T(8,128)(2,1)S(1)}, u32[]{:S(2)}, u32[]{:S(2)}) collective-permute-start(bf16[1,512,384]{2,1,0:T(8,128)(2,1)S(1)} %bitcast.136), channel_id=1, source_target_pairs={{4,0},{5,1},{6,2},{7,3},{8,4},{9,5},{10,6},{11,7},{12,8},{13,9},{1... | collective-permute-start | bytes 1179656 | tf_op jit(solution)/shard_map/ppermute | solution.py:14
  168.8 14.7 %collective-permute-start.5 = (bf16[1,512,384]{2,1,0:T(8,128)(2,1)S(1)}, bf16[1,512,384]{2,1,0:T(8,128)(2,1)S(1)}, u32[]{:S(2)}, u32[]{:S(2)}) collective-permute-start(bf16[1,512,384]{2,1,0:T(8,128)(2,1)S(1)} %bitcast.137), channel_id=1, source_target_pairs={{0,4},{1,5},{2,6},{3,7},{4,8},{5,9},{6,10},{7,11},{8,12},{9,13},{1... | collective-permute-start | bytes 1179656 | tf_op jit(solution)/shard_map/ppermute | solution.py:14
  183.4 1.7 copy-start.3
  185.1 0.9 copy-start.9
  187.6 1.1 copy-start.10
  187.6 382.8 %all-reduce.2.cloned.1.call-start = ((), (), s32[]{:S(2)}) async-start(), calls=%async_computation.3 | async-start | bytes 294912 | tf_op jit(solution)/shard_map/psum | solution.py:144
  191.5 13.3 %collective-permute-start.6 = (bf16[1,512,384]{2,1,0:T(8,128)(2,1)}, bf16[1,512,384]{2,1,0:T(8,128)(2,1)S(1)}, u32[]{:S(2)}, u32[]{:S(2)}) collective-permute-start(bf16[1,512,384]{2,1,0:T(8,128)(2,1)} %bitcast.24), channel_id=1, source_target_pairs={{2,0},{3,1},{4,2},{5,3},{6,4},{7,5},{8,6},{9,7},{10,8},{11,9},{12,... | collective-permute-start | bytes 1179656 | tf_op jit(solution)/shard_map/ppermute | solution.py:14
  193.4 68.5 %collective-permute-start.7 = (bf16[1,512,384]{2,1,0:T(8,128)(2,1)}, bf16[1,512,384]{2,1,0:T(8,128)(2,1)}, u32[]{:S(2)}, u32[]{:S(2)}) collective-permute-start(bf16[1,512,384]{2,1,0:T(8,128)(2,1)} %bitcast.24), channel_id=1, source_target_pairs={{0,2},{1,3},{2,4},{3,5},{4,6},{5,7},{6,8},{7,9},{8,10},{9,11},{10,... | collective-permute-start | bytes 1179656 | tf_op jit(solution)/shard_map/ppermute | solution.py:14
Sparse Core Ops, SparseCore 0:
  10.7 51.9 all-gather.7
  64.8 43.4 all-gather.5
  111.0 49.8 all-gather.9
  187.7 74.0 reduce-scatter.1
  264.6 305.7 all-reduce.1
where the time goes:
time: 579 us
  waiting for transfers between devices  491 us (85%)
  starting transfers between devices  32 us (6%)
  matrix products  28.3 us (5%)
  between operations  15.3 us (3%)
  local copies, waits for them, and re-layouts  6.63 us (1%)
    psum x1, waiting for transfers between devices, shards(): summed = lax.psum(shared_part, 'dp')  304 us
    all_gather x2, waiting for transfers between devices, shards(): weight = lax.all_gather(conv_weight[block_index], 'seq', axis=1, tiled=True)  78.8 us
    reduce_scatter x1, waiting for transfers between devices, shards(): lax.psum_scatter(jnp.stack([first_term, second_term], axis=1), 'seq', sca...  55.3 us
    all_gather x1, waiting for transfers between devices, shards(): point_full = lax.all_gather(point_weight, 'seq', axis=0, tiled=True)  40.6 us
    ppermute x8, starting transfers between devices, passed_along(): return lax.ppermute(value, axis, pairs)  31.8 us
    dot_general x8, matrix products, contract_last(): lax.dot_general(left, right, (((1,), (1,)), ((), ())), preferred_element_...  14.3 us
    ppermute x8, waiting for transfers between devices, passed_along(): return lax.ppermute(value, axis, pairs)  11.9 us
  transfers between devices with their start and end apart: 13, of which 7 were waited for; matrix products, arithmetic and copies ran while one was open for 5% of the time, Pallas kernels for 0%

commit v1 on v0

--- a/solution.py
+++ b/solution.py
@@ -141,7 +141,7 @@
     shared_part = lax.psum_scatter(
         jnp.stack([first_term, second_term], axis=1), "seq", scatter_dimension=0, tiled=True
     )
-    summed = lax.psum(shared_part, "dp")
+    summed = jnp.sum(lax.all_gather(shared_part, "dp"), axis=0)
     sample_count = sequence_in.shape[0] * lax.axis_size("dp")
     full_length = position_list * lax.axis_size("seq")
     point_grad = summed * (1.0 / math.sqrt(sample_count * full_length))

time: 579 us -> 447 us (0.77)
  waiting for transfers between devices: 491 us -> 360 us
    psum x1 -> x0, waiting for transfers between devices: 304 us -> none  [shards(): summed = lax.psum(shared_part, 'dp')]
    all_gather x0 -> x1, waiting for transfers between devices: none -> 153 us  [shards(): summed = jnp.sum(lax.all_gather(shared_part, 'dp'), axis=0)]
    reduce_scatter x1, waiting for transfers between devices: 55.3 us -> 74.1 us  [shards(): lax.psum_scatter(jnp.stack([first_term, second_term], axis=1), 'seq', sca...]
  transfers between devices with their start and end apart: 13 -> 13, of which waited for: 7 -> 8; matrix products, arithmetic and copies ran while one was open for 5% -> 6% of each run, Pallas kernels for 0% -> 0%
where the time goes in v1:
time: 447 us
  waiting for transfers between devices  360 us (81%)
  starting transfers between devices  34.1 us (8%)
  matrix products  23.7 us (5%)
  between operations  15.4 us (3%)
  other arithmetic  7.44 us (2%)
  local copies, waits for them, and re-layouts  5.66 us (1%)
    all_gather x1, waiting for transfers between devices, shards(): summed = jnp.sum(lax.all_gather(shared_part, 'dp'), axis=0)  153 us
    all_gather x2, waiting for transfers between devices, shards(): weight = lax.all_gather(conv_weight[block_index], 'seq', axis=1, tiled=True)  79 us
    reduce_scatter x1, waiting for transfers between devices, shards(): lax.psum_scatter(jnp.stack([first_term, second_term], axis=1), 'seq', sca...  74.1 us
    all_gather x1, waiting for transfers between devices, shards(): point_full = lax.all_gather(point_weight, 'seq', axis=0, tiled=True)  40.6 us
    ppermute x8, starting transfers between devices, passed_along(): return lax.ppermute(value, axis, pairs)  33.9 us
    ppermute x8, waiting for transfers between devices, passed_along(): return lax.ppermute(value, axis, pairs)  13.2 us
    dot_general x8, matrix products, contract_last(): lax.dot_general(left, right, (((1,), (1,)), ((), ())), preferred_element_...  9.74 us
  transfers between devices with their start and end apart: 13, of which 8 were waited for; matrix products, arithmetic and copies ran while one was open for 6% of the time, Pallas kernels for 0%

profile of v1, /device:TPU:2, one launch (start us, length us, event | category | flops | bytes accessed | tf_op | source)
XLA Modules:
  0.0 446.5 jit_solution(15876528556339746028)
XLA Ops:
  12.1 1.8 fusion.15
  13.9 7.8 %collective-permute-start.1 = (bf16[1,512,768]{2,1,0:T(8,128)(2,1)S(1)}, bf16[1,512,768]{2,1,0:T(8,128)(2,1)S(1)}, u32[]{:S(2)}, u32[]{:S(2)}) collective-permute-start(bf16[1,512,768]{2,1,0:T(8,128)(2,1)S(1)} %fusion.15), channel_id=1, source_target_pairs={{2,0},{3,1},{4,2},{5,3},{6,4},{7,5},{8,6},{9,7},{10,8},{11,9},{12,... | collective-permute-start | bytes 2359304 | tf_op jit(solution)/shard_map/ppermute | solution.py:14
  21.7 1.9 collective-permute-start
  25.0 37.8 %all-gather.10.cloned.1.call-done = bf16[1,3,768,384]{3,2,1,0:T(8,128)(2,1)} async-done(((bf16[1,3,48,384]{3,2,1,0:T(8,128)(2,1)}), bf16[1,3,768,384]{3,2,1,0:T(8,128)(2,1)}) %all-gather.10.cloned.1.call-update) | async-done | bytes 1769488 | tf_op jit(solution)/shard_map/all_gather | solution.py:98
  62.7 1.8 fusion.70
  65.1 2.7 fusion.44
  67.8 40.6 %all-gather.8.cloned.1.call-done = bf16[384,2,768]{2,0,1:T(8,128)(2,1)} async-done(((bf16[24,2,768]{2,0,1:T(8,128)(2,1)}), bf16[384,2,768]{2,0,1:T(8,128)(2,1)}) %all-gather.8.cloned.1.call-update) | async-done | bytes 1179664 | tf_op jit(solution)/shard_map/all_gather | solution.py:83
  108.3 2.0 fusion.4
  113.1 6.9 %collective-permute-start.2 = (bf16[1,512,768]{2,1,0:T(8,128)(2,1)}, bf16[1,512,768]{2,1,0:T(8,128)(2,1)}, u32[]{:S(2)}, u32[]{:S(2)}) collective-permute-start(bf16[1,512,768]{2,1,0:T(8,128)(2,1)} %fusion.102), channel_id=1, source_target_pairs={{0,4},{1,5},{2,6},{3,7},{4,8},{5,9},{6,10},{7,11},{8,12},{9,13},{1... | collective-permute-start | bytes 2359304 | tf_op jit(solution)/shard_map/ppermute | solution.py:14
  120.8 41.3 %all-gather.12.cloned.1.call-done = bf16[1,3,768,384]{3,2,1,0:T(8,128)(2,1)} async-done(((bf16[1,3,48,384]{3,2,1,0:T(8,128)(2,1)}), bf16[1,3,768,384]{3,2,1,0:T(8,128)(2,1)}) %all-gather.12.cloned.1.call-update) | async-done | bytes 1769488 | tf_op jit(solution)/shard_map/all_gather | solution.py:98
  162.1 2.0 fusion.88
  164.1 1.7 fusion.65
  165.8 1.9 fusion.41
  169.9 6.1 %collective-permute-start.5 = (bf16[1,512,384]{2,1,0:T(8,128)(2,1)S(1)}, bf16[1,512,384]{2,1,0:T(8,128)(2,1)S(1)}, u32[]{:S(2)}, u32[]{:S(2)}) collective-permute-start(bf16[1,512,384]{2,1,0:T(8,128)(2,1)S(1)} %bitcast.139), channel_id=1, source_target_pairs={{0,4},{1,5},{2,6},{3,7},{4,8},{5,9},{6,10},{7,11},{8,12},{9,13},{1... | collective-permute-start | bytes 1179656 | tf_op jit(solution)/shard_map/ppermute | solution.py:14
  177.4 6.6 %collective-permute-done.4 = bf16[1,512,384]{2,1,0:T(8,128)(2,1)S(1)} collective-permute-done((bf16[1,512,384]{2,1,0:T(8,128)(2,1)S(1)}, bf16[1,512,384]{2,1,0:T(8,128)(2,1)S(1)}, u32[]{:S(2)}, u32[]{:S(2)}) %collective-permute-start.4) | collective-permute-done | bytes 393248 | tf_op jit(solution)/shard_map/ppermute | solution.py:14
  188.8 74.1 %reduce-scatter.2.cloned.1.call-done = f32[24,2,768]{2,0,1:T(8,128)} async-done(((f32[384,2,768]{2,0,1:T(8,128)}), f32[24,2,768]{2,0,1:T(8,128)}) %reduce-scatter.2.cloned.1.call-update) | async-done | bytes 147472 | tf_op jit(solution)/shard_map/reduce_scatter | solution.py:141
  263.0 2.2 fusion.52
  265.2 6.5 %collective-permute-start.6 = (bf16[1,512,384]{2,1,0:T(8,128)(2,1)S(1)}, bf16[1,512,384]{2,1,0:T(8,128)(2,1)S(1)}, u32[]{:S(2)}, u32[]{:S(2)}) collective-permute-start(bf16[1,512,384]{2,1,0:T(8,128)(2,1)S(1)} %bitcast.140), channel_id=1, source_target_pairs={{2,0},{3,1},{4,2},{5,3},{6,4},{7,5},{8,6},{9,7},{10,8},{11,9},{12,... | collective-permute-start | bytes 1179656 | tf_op jit(solution)/shard_map/ppermute | solution.py:14
  271.7 2.1 collective-permute-start.7
  274.4 3.0 collective-permute-done.6
  278.1 3.5 collective-permute-done.7
  281.6 2.5 fusion.77
  284.1 152.5 %all-gather.14.cloned.1.call-done = f32[768,2,768]{2,0,1:T(8,128)} async-done(((f32[24,2,768]{2,0,1:T(8,128)}), f32[768,2,768]{2,0,1:T(8,128)}) %all-gather.14.cloned.1.call-update) | async-done | bytes 4718608 | tf_op jit(solution)/shard_map/all_gather | solution.py:144
  436.6 2.6 reduce_sum.9
  (59 shorter events, 19.3 us)
Async XLA Ops:
  7.2 16.5 %copy-start.7 = (s32[1,2]{1,0:T(1,128)S(1)}, s32[1,2]{1,0:T(1,128)}, u32[]{:S(2)}) copy-start(s32[1,2]{1,0:T(1,128)} %param.11) | copy-start | bytes 28
  7.2 17.7 %copy-start.6 = (f32[2,384]{1,0:T(2,128)S(1)}, f32[2,384]{1,0:T(2,128)}, u32[]{:S(2)}) copy-start(f32[2,384]{1,0:T(2,128)} %param.14) | copy-start | bytes 9220
  7.2 17.7 %copy-start.5 = (f32[2,384]{1,0:T(2,128)S(1)}, f32[2,384]{1,0:T(2,128)}, u32[]{:S(2)}) copy-start(f32[2,384]{1,0:T(2,128)} %param.15) | copy-start | bytes 9220
  7.2 55.5 %all-gather.10.cloned.1.call-start = ((), (), s32[]{:S(2)}) async-start(), calls=%async_computation.3 | async-start | bytes 1880064 | tf_op jit(solution)/shard_map/all_gather | solution.py:98
  8.9 99.4 %all-gather.8.cloned.1.call-start = ((), (), s32[]{:S(2)}) async-start(), calls=%async_computation.1 | async-start | bytes 1253376 | tf_op jit(solution)/shard_map/all_gather | solution.py:83
  10.5 151.5 %all-gather.12.cloned.1.call-start = ((), (), s32[]{:S(2)}) async-start(), calls=%async_computation.4 | async-start | bytes 1880064 | tf_op jit(solution)/shard_map/all_gather | solution.py:98
  11.3 251.7 %reduce-scatter.2.cloned.1.call-start = ((), (), s32[]{:S(2)}) async-start(), calls=%async_computation.2 | async-start | bytes 2506752 | tf_op jit(solution)/shard_map/reduce_scatter | solution.py:141
  13.9 50.6 %collective-permute-start.1 = (bf16[1,512,768]{2,1,0:T(8,128)(2,1)S(1)}, bf16[1,512,768]{2,1,0:T(8,128)(2,1)S(1)}, u32[]{:S(2)}, u32[]{:S(2)}) collective-permute-start(bf16[1,512,768]{2,1,0:T(8,128)(2,1)S(1)} %fusion.15), channel_id=1, source_target_pairs={{2,0},{3,1},{4,2},{5,3},{6,4},{7,5},{8,6},{9,7},{10,8},{11,9},{12,... | collective-permute-start | bytes 2359304 | tf_op jit(solution)/shard_map/ppermute | solution.py:14
  21.7 43.3 %collective-permute-start = (bf16[1,512,768]{2,1,0:T(8,128)(2,1)S(1)}, bf16[1,512,768]{2,1,0:T(8,128)(2,1)}, u32[]{:S(2)}, u32[]{:S(2)}) collective-permute-start(bf16[1,512,768]{2,1,0:T(8,128)(2,1)S(1)} %fusion.15), channel_id=1, source_target_pairs={{0,2},{1,3},{2,4},{3,5},{4,6},{5,7},{6,8},{7,9},{8,10},{9,11},{10,... | collective-permute-start | bytes 2359304 | tf_op jit(solution)/shard_map/ppermute | solution.py:14
  62.7 1.8 copy-start
  65.1 43.3 %copy-start.2 = (bf16[1,512,768]{2,1,0:T(8,128)(2,1)S(1)}, bf16[1,512,768]{2,1,0:T(8,128)(2,1)}, u32[]{:S(2)}) copy-start(bf16[1,512,768]{2,1,0:T(8,128)(2,1)} %param.9) | copy-start | bytes 2359300
  111.8 52.2 %collective-permute-start.3 = (bf16[1,512,768]{2,1,0:T(8,128)(2,1)}, bf16[1,512,768]{2,1,0:T(8,128)(2,1)}, u32[]{:S(2)}, u32[]{:S(2)}) collective-permute-start(bf16[1,512,768]{2,1,0:T(8,128)(2,1)} %fusion.102), channel_id=1, source_target_pairs={{4,0},{5,1},{6,2},{7,3},{8,4},{9,5},{10,6},{11,7},{12,8},{13,9},{1... | collective-permute-start | bytes 2359304 | tf_op jit(solution)/shard_map/ppermute | solution.py:14
  113.1 52.7 %collective-permute-start.2 = (bf16[1,512,768]{2,1,0:T(8,128)(2,1)}, bf16[1,512,768]{2,1,0:T(8,128)(2,1)}, u32[]{:S(2)}, u32[]{:S(2)}) collective-permute-start(bf16[1,512,768]{2,1,0:T(8,128)(2,1)} %fusion.102), channel_id=1, source_target_pairs={{0,4},{1,5},{2,6},{3,7},{4,8},{5,9},{6,10},{7,11},{8,12},{9,13},{1... | collective-permute-start | bytes 2359304 | tf_op jit(solution)/shard_map/ppermute | solution.py:14
  162.1 2.0 copy-start.1
  165.8 1.9 copy-start.8
  165.8 1.9 copy-start.9
  168.7 15.3 %collective-permute-start.4 = (bf16[1,512,384]{2,1,0:T(8,128)(2,1)S(1)}, bf16[1,512,384]{2,1,0:T(8,128)(2,1)S(1)}, u32[]{:S(2)}, u32[]{:S(2)}) collective-permute-start(bf16[1,512,384]{2,1,0:T(8,128)(2,1)S(1)} %bitcast.138), channel_id=1, source_target_pairs={{4,0},{5,1},{6,2},{7,3},{8,4},{9,5},{10,6},{11,7},{12,8},{13,9},{1... | collective-permute-start | bytes 1179656 | tf_op jit(solution)/shard_map/ppermute | solution.py:14
  169.9 14.7 %collective-permute-start.5 = (bf16[1,512,384]{2,1,0:T(8,128)(2,1)S(1)}, bf16[1,512,384]{2,1,0:T(8,128)(2,1)S(1)}, u32[]{:S(2)}, u32[]{:S(2)}) collective-permute-start(bf16[1,512,384]{2,1,0:T(8,128)(2,1)S(1)} %bitcast.139), channel_id=1, source_target_pairs={{0,4},{1,5},{2,6},{3,7},{4,8},{5,9},{6,10},{7,11},{8,12},{9,13},{1... | collective-permute-start | bytes 1179656 | tf_op jit(solution)/shard_map/ppermute | solution.py:14
  184.6 1.7 copy-start.3
  188.7 74.2 %copy-start.4 = (f32[512,384]{1,0:T(8,128)S(1)}, f32[512,384]{1,0:T(8,128)}, u32[]{:S(2)}) copy-start(f32[512,384]{1,0:T(8,128)} %fusion.44) | copy-start | bytes 2359300
  188.8 247.9 %all-gather.14.cloned.1.call-start = ((), (), s32[]{:S(2)}) async-start(), calls=%async_computation.5 | async-start | bytes 4866048 | tf_op jit(solution)/shard_map/all_gather | solution.py:144
  265.2 12.2 %collective-permute-start.6 = (bf16[1,512,384]{2,1,0:T(8,128)(2,1)S(1)}, bf16[1,512,384]{2,1,0:T(8,128)(2,1)S(1)}, u32[]{:S(2)}, u32[]{:S(2)}) collective-permute-start(bf16[1,512,384]{2,1,0:T(8,128)(2,1)S(1)} %bitcast.140), channel_id=1, source_target_pairs={{2,0},{3,1},{4,2},{5,3},{6,4},{7,5},{8,6},{9,7},{10,8},{11,9},{12,... | collective-permute-start | bytes 1179656 | tf_op jit(solution)/shard_map/ppermute | solution.py:14
  271.7 9.8 %collective-permute-start.7 = (bf16[1,512,384]{2,1,0:T(8,128)(2,1)S(1)}, bf16[1,512,384]{2,1,0:T(8,128)(2,1)S(1)}, u32[]{:S(2)}, u32[]{:S(2)}) collective-permute-start(bf16[1,512,384]{2,1,0:T(8,128)(2,1)S(1)} %bitcast.141), channel_id=1, source_target_pairs={{0,2},{1,3},{2,4},{3,5},{4,6},{5,7},{6,8},{7,9},{8,10},{9,11},{10,... | collective-permute-start | bytes 1179656 | tf_op jit(solution)/shard_map/ppermute | solution.py:14
  274.4 7.1 %copy-start.11 = (bf16[512,768]{1,0:T(8,128)(2,1)S(1)}, bf16[512,768]{1,0:T(8,128)(2,1)}, u32[]{:S(2)}) copy-start(bf16[512,768]{1,0:T(8,128)(2,1)} %copy-done.10) | copy-start | bytes 2359300
  (1 other events, 0.9 us)
Sparse Core Ops, SparseCore 0:
  10.7 51.9 all-gather.9
  64.8 43.4 all-gather.7
  111.0 51.0 all-gather.11
  188.9 74.0 reduce-scatter.1
  265.9 170.6 all-gather.13
